TPU v7x, 32 devices: a whole 2x2x4 slice. The times are simulated.
32 devices in a mesh: tm: 8 (over z, x), pack: 4 (over y, core).
Axes of the slice: x: 2, y: 2, z: 4, core: 2. Of those that a mesh axis runs over, the one named last changes fastest.
Arguments:
- queries: bfloat16 [4, 4096, 1024], P('pack', 'tm'), may hold values from -8 to 8
- keys: bfloat16 [4, 4096, 1024], P('pack', 'tm'), may hold values from -8 to 8
- values: bfloat16 [4, 4096, 1024], P('pack', 'tm'), may hold values from -6 to 6
- w_out: bfloat16 [1024, 1024], replicated, may hold values from -0.1875 to 0.1875
- norm_gain: float32 [1024], replicated, may hold values from 0.1 to 1.9
- block_owner: int32 [4, 32, 1], P('pack', 'tm'), may hold values from 0 to 3; in each aligned block of 4 rows (0 to 3, 4 to 7, ..., all dimensions but the last counted through in order) at most 2 rows name the same one
- block_base: int32 [4, 32], P('pack', 'tm'), may hold values from 0 to 112
- frame_offset: int32 [4, 32, 128], P('pack', 'tm'), may hold values from 0 to 15, never falling along the last dimension, each value on 1 to 16 neighbouring positions
Outputs:
- encoded: bfloat16 [4, 4096, 1024], P('pack', 'tm')
- pooled: bfloat16 [4, 1024, 1024], P('pack', 'tm')
Inputs may be any that keep to these rules, and one draw needn't show every extreme that they name: `block_owner`: among the 4 blocks of one device (aligned runs of the list), at most 2 name the same owner. `frame_offset`: within each block of 128 frames the offsets never fall and each of 0 to 15 occurs.
All inputs are finite; a program needn't handle non-finite values.
Results may differ from a plain program's by a relative error of at most 0.008.
Values may be sent and summed in bfloat16 or wider, within the bound.
No kernel may reach another device: no remote copies, remote signals or barrier semaphores. Data moves between devices by JAX's collectives and lax.ppermute only.
A program may use at most 128 MiB of HBM per device.

v0:
```python
import math
import jax
import jax.numpy as jnp
from jax import lax
from jax.sharding import PartitionSpec as P

HEADS = 16
LANDMARKS = 256
BLOCK = 128
POOL_DEV = 128


def mix_heads(query_rows, mark_keys, mark_values, head_count):
    row_count, model_width = query_rows.shape
    head_dim = model_width // head_count
    query_heads = query_rows.reshape(row_count, head_count, head_dim)
    key_heads = mark_keys.reshape(-1, head_count, head_dim)
    value_heads = mark_values.reshape(-1, head_count, head_dim)
    scores = jnp.einsum(
        "nhe,mhe->nhm", query_heads, key_heads, preferred_element_type=jnp.float32
    ) * head_dim ** (-0.5)
    weights = jnp.exp(scores - jnp.max(scores, axis=-1, keepdims=True))
    totals = jnp.sum(weights, axis=-1)
    blended = jnp.einsum(
        "nhm,mhe->nhe",
        weights.astype(jnp.bfloat16),
        value_heads,
        preferred_element_type=jnp.float32,
    )
    return (blended / totals[..., None]).reshape(row_count, model_width).astype(jnp.bfloat16)


def mix_blocked(query_rows, mark_keys, mark_values, head_count):
    row_count, model_width = query_rows.shape
    row_block = math.gcd(row_count, 1024)
    stacked = query_rows.reshape(row_count // row_block, row_block, model_width)
    mixed_rows = lax.map(
        lambda frame_block: mix_heads(frame_block, mark_keys, mark_values, head_count), stacked
    )
    return mixed_rows.reshape(row_count, model_width)


def local(queries, keys, values, w_out, norm_gain, block_owner, block_base, frame_offset):
    frame_q = queries[0]
    frame_k = keys[0]
    frame_v = values[0]
    frame_count, model_width = frame_q.shape
    span = frame_count // LANDMARKS
    mark_queries = jnp.mean(
        frame_q.reshape(LANDMARKS, span, model_width), axis=1, dtype=jnp.float32
    ).astype(jnp.bfloat16)
    mark_keys = jnp.mean(
        frame_k.reshape(LANDMARKS, span, model_width), axis=1, dtype=jnp.float32
    ).astype(jnp.bfloat16)
    mark_values = mix_heads(mark_queries, frame_k, frame_v, HEADS)
    spread_q, spread_k, spread_v = (
        lax.all_to_all(frame_q, "tm", split_axis=1, concat_axis=0, tiled=True),
        lax.all_to_all(mark_keys, "tm", split_axis=1, concat_axis=0, tiled=True),
        lax.all_to_all(mark_values, "tm", split_axis=1, concat_axis=0, tiled=True),
    )
    local_heads = HEADS // lax.axis_size("tm")
    head_result = mix_blocked(spread_q, spread_k, spread_v, local_heads)
    attended = lax.all_to_all(head_result, "tm", split_axis=0, concat_axis=1, tiled=True)
    projected = jnp.dot(attended, w_out, preferred_element_type=jnp.float32)
    scaled = projected * lax.rsqrt(jnp.mean(projected * projected, axis=-1, keepdims=True) + 1e-06)
    encoded = (scaled * norm_gain).astype(jnp.bfloat16)
    pack_count = lax.axis_size("pack")
    owners = block_owner[0, :, 0]
    block_count = owners.shape[0]
    slot_count = max(2, 2 * block_count // pack_count)
    pack_range = jnp.arange(pack_count, dtype=jnp.int32)
    dest_hits = (owners[:, None] == pack_range[None, :]).astype(jnp.int32)
    slot_rank = jnp.sum((jnp.cumsum(dest_hits, axis=0) - dest_hits) * dest_hits, axis=1)
    chosen = (owners[None, None, :] == pack_range[:, None, None]) & (
        slot_rank[None, None, :] == jnp.arange(slot_count, dtype=jnp.int32)[None, :, None]
    )
    filled = jnp.any(chosen, axis=-1)
    source_block = jnp.sum(
        chosen.astype(jnp.int32) * jnp.arange(block_count, dtype=jnp.int32)[None, None, :], axis=-1
    )
    frame_blocks = encoded.reshape(block_count, BLOCK, model_width)
    offsets = frame_offset[0]
    block_bases = block_base[0]
    sent_rows = jnp.where(
        filled[..., None, None],
        jnp.take(frame_blocks, source_block, axis=0),
        jnp.zeros((), jnp.bfloat16),
    )
    row_targets = jnp.take(block_bases, source_block)[..., None] + jnp.take(
        offsets, source_block, axis=0
    )
    sent_targets = jnp.where(filled[..., None], row_targets, -1).astype(jnp.bfloat16)
    got_rows, got_targets = (
        lax.all_to_all(sent_rows, "pack", split_axis=0, concat_axis=0, tiled=True),
        lax.all_to_all(sent_targets, "pack", split_axis=0, concat_axis=0, tiled=True),
    )
    pool_rows = jnp.arange(POOL_DEV, dtype=jnp.int32).astype(jnp.bfloat16)
    placing = got_targets[:, :, None, :] == pool_rows[None, None, :, None]
    pool_sums = jnp.einsum(
        "scrf,scfd->rd", placing.astype(jnp.bfloat16), got_rows, preferred_element_type=jnp.float32
    )
    pool_counts = jnp.sum(placing.astype(jnp.float32), axis=(0, 1, 3))
    pooled = (pool_sums / jnp.maximum(pool_counts, 1.0)[:, None]).astype(jnp.bfloat16)
    return (encoded[None], pooled[None])


def solution(mesh):
    return jax.shard_map(
        local,
        mesh=mesh,
        in_specs=(
            P("pack", "tm", None),
            P("pack", "tm", None),
            P("pack", "tm", None),
            P(),
            P(),
            P("pack", "tm", None),
            P("pack", "tm"),
            P("pack", "tm", None),
        ),
        out_specs=(P("pack", "tm", None), P("pack", "tm", None)),
        check_vma=False,
    )
```

profile of v0, /device:TPU:0, one launch (start us, length us, event | category | flops | bytes accessed | tf_op | source)
XLA Modules:
  0.0 267.6 jit_solution(12814046430353551243)
XLA Ops:
  0.7 3.6 %reshape.165 = f32[256,2,1024]{2,1,0:T(2,128)} reshape(bf16[1,512,1024]{2,1,0:T(8,128)(2,1)} %param.11) | data formatting | bytes 3145728 | tf_op jit(solution)/shard_map/convert_element_type | solution.py:52
  4.2 5.1 %reduce_sum.74 = f32[256,1024]{1,0:T(8,128)} reduce(f32[256,2,1024]{2,1,0:T(2,128)} %reshape.165, f32[]{:T(128)} %constant.55.clone.1), dimensions={1}, to_apply=%region_0.0 | reduce | flops 262144 | bytes 3145732 | tf_op jit(solution)/shard_map/reduce_sum | solution.py:52
  13.5 7.3 %all-to-all-start.1 = ((bf16[256,8,128]{0,2,1:T(8,128)(2,1)}), bf16[256,8,128]{0,2,1:T(8,128)(2,1)}, u32[]{:S(2)}, u32[]{:S(2)}) async-start(bf16[256,8,128]{0,2,1:T(8,128)(2,1)} %bitcast.126), calls=%async_computation.1 | async-start | bytes 1048576 | tf_op jit(solution)/shard_map/all_to_all | solution.py:58
  22.1 3.5 %reshape.166 = f32[256,2,1024]{2,1,0:T(2,128)} reshape(bf16[1,512,1024]{2,1,0:T(8,128)(2,1)} %param.10) | data formatting | bytes 3145728 | tf_op jit(solution)/shard_map/convert_element_type | solution.py:49
  25.6 5.1 %reduce_sum.75 = f32[256,1024]{1,0:T(8,128)} reduce(f32[256,2,1024]{2,1,0:T(2,128)} %reshape.166, f32[]{:T(128)} %constant.55.clone.1), dimensions={1}, to_apply=%region_1.0 | reduce | flops 262144 | bytes 3145732 | tf_op jit(solution)/shard_map/reduce_sum | solution.py:49
  44.8 6.1 %divide_convert_fusion = bf16[256,16,64]{0,2,1:T(8,128)(2,1)} fusion(bf16[512,16,64]{0,2,1:T(8,128)(2,1)} %bitcast.129, f32[16,256,512]{2,1,0:T(8,128)} %copy-done.3, f32[256,16]{0,1:T(8,128)S(1)} %get-tuple-element.71, f32[256,16]{0,1:T(8,128)S(1)} %fusion.16), kind=kOutput, calls=%fused_computation.30 | convolution fusion | flops 275251200 | bytes 9994240 | tf_op jit(solution)/shard_map/nhm,mhe->nhe/dot_general | solution.py:24
  51.0 6.0 %all-to-all-start.2 = ((bf16[256,8,128]{0,2,1:T(8,128)(2,1)}), bf16[256,8,128]{0,2,1:T(8,128)(2,1)}, u32[]{:S(2)}, u32[]{:S(2)}) async-start(bf16[256,8,128]{0,2,1:T(8,128)(2,1)} %bitcast.131), calls=%async_computation.2 | async-start | bytes 1048576 | tf_op jit(solution)/shard_map/all_to_all | solution.py:59
  58.3 12.7 %all-to-all-done.2 = bf16[256,8,128]{0,2,1:T(8,128)(2,1)} async-done(((bf16[256,8,128]{0,2,1:T(8,128)(2,1)}), bf16[256,8,128]{0,2,1:T(8,128)(2,1)}, u32[]{:S(2)}, u32[]{:S(2)}) %all-to-all-start.2) | async-done | bytes 524320 | tf_op jit(solution)/shard_map/all_to_all | solution.py:59
  71.0 4.2 %all-to-all-start = ((bf16[512,8,128]{0,2,1:T(8,128)(2,1)}), bf16[512,8,128]{0,2,1:T(8,128)(2,1)}, u32[]{:S(2)}, u32[]{:S(2)}) async-start(bf16[512,8,128]{0,2,1:T(8,128)(2,1)} %bitcast.124), calls=%async_computation | async-start | bytes 2097152 | tf_op jit(solution)/shard_map/all_to_all | solution.py:57
  78.8 21.8 %all-to-all-done = bf16[512,8,128]{0,2,1:T(8,128)(2,1)} async-done(((bf16[512,8,128]{0,2,1:T(8,128)(2,1)}), bf16[512,8,128]{0,2,1:T(8,128)(2,1)}, u32[]{:S(2)}, u32[]{:S(2)}) %all-to-all-start) | async-done | bytes 1048608 | tf_op jit(solution)/shard_map/all_to_all | solution.py:57
  102.8 89.4 %while.10 = (s32[]{:T(128)}, bf16[4,1024,128]{2,1,0:T(8,128)(2,1)}, bf16[4,1024,128]{2,1,0:T(8,128)(2,1)}, bf16[2048,128]{0,1:T(8,128)(2,1)S(1)}, bf16[2048,128]{0,1:T(8,128)(2,1)}, /*index=5*/s32[]{:T(128)}) while((s32[]{:T(128)}, bf16[4,1024,128]{2,1,0:T(8,128)(2,1)}, bf16[4,1024,128]{2,1,0:T(8,128)(2,1)}, bf16[2048,128]{0,1:T(8,128)(2,1)S(1)}, ...), condition=%wide.region_7.8_spmd, body=%wide.region_4.7_spmd.sunk | while | flops 1107554304 | bytes 121151608 | solution.py:37
  106.5 5.7 %copy-done.2 = f32[2,1024,2048]{2,1,0:T(8,128)} copy-done((f32[2,1024,2048]{2,1,0:T(8,128)}, f32[2,1024,2048]{2,1,0:T(8,128)S(1)}, u32[]{:S(2)}) %copy-start.2) | copy-done | bytes 16777240 | tf_op jit(solution)/shard_map/while
  115.4 8.9 %fusion.68 = bf16[1024,2,64]{0,2,1:T(8,128)(2,1)S(1)} fusion(bf16[2048,2,64]{0,2,1:T(8,128)(2,1)} %bitcast.110, f32[2,1024,2048]{2,1,0:T(8,128)} %copy-done.2, f32[1024,2]{0,1:T(2,128)S(1)} %get-tuple-element.109, f32[1024,2]{0,1:T(2,128)S(1)} %fusion.67), kind=kOutput, calls=%fused_computation.11.clone.1 | convolution fusion | flops 549715968 | bytes 17580032 | tf_op jit(solution)/shard_map/while/body/eval_jaxpr/nhm,mhe->nhe/dot_general | solution.py:24
  128.8 5.7 %copy-done.2 = f32[2,1024,2048]{2,1,0:T(8,128)} copy-done((f32[2,1024,2048]{2,1,0:T(8,128)}, f32[2,1024,2048]{2,1,0:T(8,128)S(1)}, u32[]{:S(2)}) %copy-start.2) | copy-done | bytes 16777240 | tf_op jit(solution)/shard_map/while
  134.5 3.3 %fusion.67 = f32[1024,2]{0,1:T(2,128)S(1)} fusion(f32[2,1024,2048]{2,1,0:T(8,128)S(1)} %get-tuple-element.108, f32[1024,2]{0,1:T(2,128)S(1)} %get-tuple-element.109), kind=kLoop, calls=%fused_computation.6.clone.1 | loop fusion | flops 12580864 | bytes 16793600 | tf_op jit(solution)/shard_map/while/body/eval_jaxpr/reduce_sum | solution.py:23
  137.8 8.8 %fusion.68 = bf16[1024,2,64]{0,2,1:T(8,128)(2,1)S(1)} fusion(bf16[2048,2,64]{0,2,1:T(8,128)(2,1)} %bitcast.110, f32[2,1024,2048]{2,1,0:T(8,128)} %copy-done.2, f32[1024,2]{0,1:T(2,128)S(1)} %get-tuple-element.109, f32[1024,2]{0,1:T(2,128)S(1)} %fusion.67), kind=kOutput, calls=%fused_computation.11.clone.1 | convolution fusion | flops 549715968 | bytes 17580032 | tf_op jit(solution)/shard_map/while/body/eval_jaxpr/nhm,mhe->nhe/dot_general | solution.py:24
  151.1 5.7 %copy-done.2 = f32[2,1024,2048]{2,1,0:T(8,128)} copy-done((f32[2,1024,2048]{2,1,0:T(8,128)}, f32[2,1024,2048]{2,1,0:T(8,128)S(1)}, u32[]{:S(2)}) %copy-start.2) | copy-done | bytes 16777240 | tf_op jit(solution)/shard_map/while
  160.1 8.8 %fusion.68 = bf16[1024,2,64]{0,2,1:T(8,128)(2,1)S(1)} fusion(bf16[2048,2,64]{0,2,1:T(8,128)(2,1)} %bitcast.110, f32[2,1024,2048]{2,1,0:T(8,128)} %copy-done.2, f32[1024,2]{0,1:T(2,128)S(1)} %get-tuple-element.109, f32[1024,2]{0,1:T(2,128)S(1)} %fusion.67), kind=kOutput, calls=%fused_computation.11.clone.1 | convolution fusion | flops 549715968 | bytes 17580032 | tf_op jit(solution)/shard_map/while/body/eval_jaxpr/nhm,mhe->nhe/dot_general | solution.py:24
  173.5 5.7 %copy-done.2 = f32[2,1024,2048]{2,1,0:T(8,128)} copy-done((f32[2,1024,2048]{2,1,0:T(8,128)}, f32[2,1024,2048]{2,1,0:T(8,128)S(1)}, u32[]{:S(2)}) %copy-start.2) | copy-done | bytes 16777240 | tf_op jit(solution)/shard_map/while
  182.4 8.8 %fusion.68 = bf16[1024,2,64]{0,2,1:T(8,128)(2,1)S(1)} fusion(bf16[2048,2,64]{0,2,1:T(8,128)(2,1)} %bitcast.110, f32[2,1024,2048]{2,1,0:T(8,128)} %copy-done.2, f32[1024,2]{0,1:T(2,128)S(1)} %get-tuple-element.109, f32[1024,2]{0,1:T(2,128)S(1)} %fusion.67), kind=kOutput, calls=%fused_computation.11.clone.1 | convolution fusion | flops 549715968 | bytes 17580032 | tf_op jit(solution)/shard_map/while/body/eval_jaxpr/nhm,mhe->nhe/dot_general | solution.py:24
  192.2 3.7 %all-to-all-start.3 = ((bf16[8,512,128]{2,1,0:T(8,128)(2,1)}), bf16[8,512,128]{2,1,0:T(8,128)(2,1)S(1)}, u32[]{:S(2)}, u32[]{:S(2)}) async-start(bf16[8,512,128]{2,1,0:T(8,128)(2,1)} %bitcast.128), calls=%async_computation.3 | async-start | bytes 2097152 | tf_op jit(solution)/shard_map/all_to_all | solution.py:63
  199.1 22.5 %all-to-all-done.3 = bf16[8,512,128]{2,1,0:T(8,128)(2,1)S(1)} async-done(((bf16[8,512,128]{2,1,0:T(8,128)(2,1)}), bf16[8,512,128]{2,1,0:T(8,128)(2,1)S(1)}, u32[]{:S(2)}, u32[]{:S(2)}) %all-to-all-start.3) | async-done | bytes 1048608 | tf_op jit(solution)/shard_map/all_to_all | solution.py:63
  234.6 4.4 %all-to-all-start.5 = ((bf16[4,2,128,1024]{3,2,1,0:T(8,128)(2,1)}), bf16[4,2,128,1024]{3,2,1,0:T(8,128)(2,1)}, u32[]{:S(2)}, u32[]{:S(2)}) async-start(bf16[4,2,128,1024]{3,2,1,0:T(8,128)(2,1)} %select_select_fusion), calls=%async_computation.5 | async-start | bytes 4194304 | tf_op jit(solution)/shard_map/all_to_all | solution.py:94
  242.1 22.7 %all-to-all-done.5 = bf16[4,2,128,1024]{3,2,1,0:T(8,128)(2,1)} async-done(((bf16[4,2,128,1024]{3,2,1,0:T(8,128)(2,1)}), bf16[4,2,128,1024]{3,2,1,0:T(8,128)(2,1)}, u32[]{:S(2)}, u32[]{:S(2)}) %all-to-all-start.5) | async-done | bytes 2097184 | tf_op jit(solution)/shard_map/all_to_all | solution.py:94
  (97 shorter events, 76.5 us)
Async XLA Ops:
  0.6 225.8 %copy-start = (bf16[1024,1024]{1,0:T(8,128)(2,1)S(1)}, bf16[1024,1024]{1,0:T(8,128)(2,1)}, u32[]{:S(2)}) copy-start(bf16[1024,1024]{1,0:T(8,128)(2,1)} %param.13) | copy-start | bytes 6291460
  0.6 20.1 %copy-start.5 = (bf16[1,512,1024]{2,1,0:T(8,128)(2,1)S(1)}, bf16[1,512,1024]{2,1,0:T(8,128)(2,1)}, u32[]{:S(2)}) copy-start(bf16[1,512,1024]{2,1,0:T(8,128)(2,1)} %param.11) | copy-start | bytes 3145732
  13.5 37.5 %all-to-all-start.1 = ((bf16[256,8,128]{0,2,1:T(8,128)(2,1)}), bf16[256,8,128]{0,2,1:T(8,128)(2,1)}, u32[]{:S(2)}, u32[]{:S(2)}) async-start(bf16[256,8,128]{0,2,1:T(8,128)(2,1)} %bitcast.126), calls=%async_computation.1 | async-start | bytes 1048576 | tf_op jit(solution)/shard_map/all_to_all | solution.py:58
  22.1 12.7 %copy-start.7 = (bf16[1,512,1024]{1,2,0:T(8,128)(2,1)S(1)}, bf16[1,512,1024]{1,2,0:T(8,128)(2,1)}, u32[]{:S(2)}) copy-start(bf16[1,512,1024]{1,2,0:T(8,128)(2,1)} %copy.83) | copy-start | bytes 3145732
  37.2 3.2 %copy-start.3 = (f32[16,256,512]{2,1,0:T(8,128)}, f32[16,256,512]{2,1,0:T(8,128)S(1)}, u32[]{:S(2)}) copy-start(f32[16,256,512]{2,1,0:T(8,128)S(1)} %get-tuple-element.72) | copy-start | bytes 25165828
  42.5 14.5 %copy-start.6 = (bf16[1,512,1024]{2,1,0:T(8,128)(2,1)S(1)}, bf16[1,512,1024]{2,1,0:T(8,128)(2,1)}, u32[]{:S(2)}) copy-start(bf16[1,512,1024]{2,1,0:T(8,128)(2,1)} %param.10) | copy-start | bytes 3145732
  51.0 20.1 %all-to-all-start.2 = ((bf16[256,8,128]{0,2,1:T(8,128)(2,1)}), bf16[256,8,128]{0,2,1:T(8,128)(2,1)}, u32[]{:S(2)}, u32[]{:S(2)}) async-start(bf16[256,8,128]{0,2,1:T(8,128)(2,1)} %bitcast.131), calls=%async_computation.2 | async-start | bytes 1048576 | tf_op jit(solution)/shard_map/all_to_all | solution.py:59
  71.0 29.5 %all-to-all-start = ((bf16[512,8,128]{0,2,1:T(8,128)(2,1)}), bf16[512,8,128]{0,2,1:T(8,128)(2,1)}, u32[]{:S(2)}, u32[]{:S(2)}) async-start(bf16[512,8,128]{0,2,1:T(8,128)(2,1)} %bitcast.124), calls=%async_computation | async-start | bytes 2097152 | tf_op jit(solution)/shard_map/all_to_all | solution.py:57
  102.8 93.1 %copy-start.11 = (s32[1,4,1]{1,2,0:T(1,128)S(1)}, s32[1,4,1]{1,2,0:T(1,128)}, u32[]{:S(2)}) copy-start(s32[1,4,1]{1,2,0:T(1,128)} %param.15) | copy-start | bytes 52
  102.8 93.8 %copy-start.1 = (s32[1,4]{1,0:T(1,128)S(1)}, s32[1,4]{1,0:T(1,128)}, u32[]{:S(2)}) copy-start(s32[1,4]{1,0:T(1,128)} %param.16) | copy-start | bytes 52
  102.8 95.0 %copy-start.9 = (s32[1,4,128]{2,1,0:T(4,128)S(1)}, s32[1,4,128]{2,1,0:T(4,128)}, u32[]{:S(2)}) copy-start(s32[1,4,128]{2,1,0:T(4,128)} %param.17) | copy-start | bytes 6148
  106.5 5.7 %copy-start.2 = (f32[2,1024,2048]{2,1,0:T(8,128)}, f32[2,1024,2048]{2,1,0:T(8,128)S(1)}, u32[]{:S(2)}) copy-start(f32[2,1024,2048]{2,1,0:T(8,128)S(1)} %get-tuple-element.108) | copy-start | bytes 50331652 | tf_op jit(solution)/shard_map/while
  128.8 5.7 %copy-start.2 = (f32[2,1024,2048]{2,1,0:T(8,128)}, f32[2,1024,2048]{2,1,0:T(8,128)S(1)}, u32[]{:S(2)}) copy-start(f32[2,1024,2048]{2,1,0:T(8,128)S(1)} %get-tuple-element.108) | copy-start | bytes 50331652 | tf_op jit(solution)/shard_map/while
  151.1 5.7 %copy-start.2 = (f32[2,1024,2048]{2,1,0:T(8,128)}, f32[2,1024,2048]{2,1,0:T(8,128)S(1)}, u32[]{:S(2)}) copy-start(f32[2,1024,2048]{2,1,0:T(8,128)S(1)} %get-tuple-element.108) | copy-start | bytes 50331652 | tf_op jit(solution)/shard_map/while
  173.5 5.7 %copy-start.2 = (f32[2,1024,2048]{2,1,0:T(8,128)}, f32[2,1024,2048]{2,1,0:T(8,128)S(1)}, u32[]{:S(2)}) copy-start(f32[2,1024,2048]{2,1,0:T(8,128)S(1)} %get-tuple-element.108) | copy-start | bytes 50331652 | tf_op jit(solution)/shard_map/while
  192.2 36.9 %copy-start.10 = (f32[1024]{0:T(1024)S(1)}, f32[1024]{0:T(1024)}, u32[]{:S(2)}) copy-start(f32[1024]{0:T(1024)} %param.14) | copy-start | bytes 12292
  192.2 29.5 %all-to-all-start.3 = ((bf16[8,512,128]{2,1,0:T(8,128)(2,1)}), bf16[8,512,128]{2,1,0:T(8,128)(2,1)S(1)}, u32[]{:S(2)}, u32[]{:S(2)}) async-start(bf16[8,512,128]{2,1,0:T(8,128)(2,1)} %bitcast.128), calls=%async_computation.3 | async-start | bytes 2097152 | tf_op jit(solution)/shard_map/all_to_all | solution.py:63
  221.7 3.2 %copy-start.8 = (bf16[8,512,128]{2,1,0:T(8,128)(2,1)}, bf16[8,512,128]{2,1,0:T(8,128)(2,1)S(1)}, u32[]{:S(2)}) copy-start(bf16[8,512,128]{2,1,0:T(8,128)(2,1)S(1)} %all-to-all-done.3) | copy-start | bytes 3145732
  221.7 12.9 %all-to-all-start.4 = ((bf16[4,2,128]{2,1,0:T(2,128)(2,1)}), bf16[4,2,128]{2,1,0:T(2,128)(2,1)S(1)}, u32[]{:S(2)}, u32[]{:S(2)}) async-start(bf16[4,2,128]{2,1,0:T(2,128)(2,1)} %select_convert_fusion), calls=%async_computation.4 | async-start | bytes 4096 | tf_op jit(solution)/shard_map/all_to_all | solution.py:95
  227.8 1.4 copy-start.4
  234.6 30.2 %all-to-all-start.5 = ((bf16[4,2,128,1024]{3,2,1,0:T(8,128)(2,1)}), bf16[4,2,128,1024]{3,2,1,0:T(8,128)(2,1)}, u32[]{:S(2)}, u32[]{:S(2)}) async-start(bf16[4,2,128,1024]{3,2,1,0:T(8,128)(2,1)} %select_select_fusion), calls=%async_computation.5 | async-start | bytes 4194304 | tf_op jit(solution)/shard_map/all_to_all | solution.py:94
where the time goes:
time: 269 us; the launch traced here: 268 us
  waiting for transfers between devices  79.7 us (30%)
  local copies, waits for them, and re-layouts  62.9 us (23%)
  matrix products  58 us (22%)
  other arithmetic  37.1 us (14%)
  starting transfers between devices  28.9 us (11%)
    dot_general x5, matrix products, mix_heads(): jnp.einsum('nhm,mhe->nhe', weights.astype(jnp.bfloat16), value_heads, pre...  41.5 us
    while x8, local copies, waits for them, and re-layouts  22.9 us
    all_to_all x1, waiting for transfers between devices, local(): lax.all_to_all(sent_rows, 'pack', split_axis=0, concat_axis=0, tiled=True)  22.7 us
    all_to_all x1, waiting for transfers between devices, local(): lax.all_to_all(head_result, 'tm', split_axis=0, concat_axis=1, tiled=True)  22.5 us
    all_to_all x1, waiting for transfers between devices, local(): lax.all_to_all(frame_q, 'tm', split_axis=1, concat_axis=0, tiled=True)  21.8 us
    reduce_sum x5, other arithmetic, mix_heads(): totals = jnp.sum(weights, axis=-1)  15 us
    all_to_all x1, waiting for transfers between devices, local(): lax.all_to_all(mark_values, 'tm', split_axis=1, concat_axis=0, tiled=True)  12.7 us
    dot_general x5, matrix products, mix_heads(): jnp.einsum('nhe,mhe->nhm', query_heads, key_heads, preferred_element_type...  12.3 us
  transfers between devices with their start and end apart: 6, of which 4 were waited for; matrix products, arithmetic and copies ran while one was open for 17% of the time, Pallas kernels for 0%

commit v1 on v0

--- a/solution.py
+++ b/solution.py
@@ -8,6 +8,29 @@
 LANDMARKS = 256
 BLOCK = 128
 POOL_DEV = 128
+
+
+def split_up(shard, dim, devices):
+    dims = shard.shape
+    blocks = shard.reshape(*dims[:dim], devices, dims[dim] // devices, *dims[dim + 1 :])
+    return jnp.moveaxis(blocks, dim, 0)
+
+
+def in_order(tiles, dim):
+    shape = list(tiles.shape[1:])
+    shape[dim] *= tiles.shape[0]
+    return jnp.moveaxis(tiles, 0, dim).reshape(shape)
+
+
+def sent_to_each(x, axis, split_dim, concat_dim):
+    size, position = (lax.axis_size(axis), lax.axis_index(axis))
+    blocks = split_up(x, split_dim, size)
+    outs = [blocks[position]]
+    for lap in range(1, size):
+        sent = blocks[(position + lap) % size]
+        outs.append(lax.ppermute(sent, axis, [(i, (i + lap) % size) for i in range(size)]))
+    blocks = jnp.stack(outs)[(position - jnp.arange(size)) % size]
+    return in_order(blocks, concat_dim)
 
 
 def mix_heads(query_rows, mark_keys, mark_values, head_count):
@@ -56,7 +79,7 @@
     spread_q, spread_k, spread_v = (
         lax.all_to_all(frame_q, "tm", split_axis=1, concat_axis=0, tiled=True),
         lax.all_to_all(mark_keys, "tm", split_axis=1, concat_axis=0, tiled=True),
-        lax.all_to_all(mark_values, "tm", split_axis=1, concat_axis=0, tiled=True),
+        sent_to_each(mark_values, "tm", 1, 0),
     )
     local_heads = HEADS // lax.axis_size("tm")
     head_result = mix_blocked(spread_q, spread_k, spread_v, local_heads)

time: 269 us -> 254 us (0.944)
  waiting for transfers between devices: 79.7 us -> 56 us
  starting transfers between devices: 28.9 us -> 42.1 us
  local copies, waits for them, and re-layouts: 62.9 us -> 58.5 us
    all_to_all x1, waiting for transfers between devices: 21.8 us -> 3.57 us  [local(): lax.all_to_all(frame_q, 'tm', split_axis=1, concat_axis=0, tiled=True)]
    ppermute x0 -> x7, starting transfers between devices: none -> 15.1 us  [sent_to_each(): lax.ppermute(sent, axis, [(i, (i + lap) % size) for i in range(size)])]
    while x8, local copies, waits for them, and re-layouts: 22.9 us -> 9.79 us
    all_to_all x1 -> x0, waiting for transfers between devices: 12.7 us -> none  [local(): lax.all_to_all(mark_values, 'tm', split_axis=1, concat_axis=0, tiled=True)]
    ppermute x0 -> x7, waiting for transfers between devices: none -> 9.34 us  [sent_to_each(): lax.ppermute(sent, axis, [(i, (i + lap) % size) for i in range(size)])]
    another operation x0 -> x11, local copies, waits for them, and re-layouts: none -> 6.2 us
    all_to_all x1 -> x0, starting transfers between devices: 5.99 us -> none  [local(): lax.all_to_all(mark_values, 'tm', split_axis=1, concat_axis=0, tiled=True)]
    all_to_all x1, starting transfers between devices: 3.69 us -> 7.89 us  [local(): lax.all_to_all(head_result, 'tm', split_axis=0, concat_axis=1, tiled=True)]
  transfers between devices with their start and end apart: 6 -> 12, of which waited for: 4 -> 5; matrix products, arithmetic and copies ran while one was open for 17% -> 21% of each run, Pallas kernels for 0% -> 0%
where the time goes in v1:
time: 254 us; the launch traced here: 252 us
  local copies, waits for them, and re-layouts  58.5 us (23%)
  matrix products  57.2 us (23%)
  waiting for transfers between devices  56 us (22%)
  starting transfers between devices  42.1 us (17%)
  other arithmetic  37.1 us (15%)
    dot_general x5, matrix products, mix_heads(): jnp.einsum('nhm,mhe->nhe', weights.astype(jnp.bfloat16), value_heads, pre...  40.7 us
    all_to_all x1, waiting for transfers between devices, local(): lax.all_to_all(sent_rows, 'pack', split_axis=0, concat_axis=0, tiled=True)  22.7 us
    all_to_all x1, waiting for transfers between devices, local(): lax.all_to_all(head_result, 'tm', split_axis=0, concat_axis=1, tiled=True)  20.4 us
    reduce_sum x5, other arithmetic, mix_heads(): totals = jnp.sum(weights, axis=-1)  15.1 us
    ppermute x7, starting transfers between devices, sent_to_each(): lax.ppermute(sent, axis, [(i, (i + lap) % size) for i in range(size)])  15.1 us
    unnamed x34, local copies, waits for them, and re-layouts  13.1 us
    dot_general x5, matrix products, mix_heads(): jnp.einsum('nhe,mhe->nhm', query_heads, key_heads, preferred_element_type...  12.3 us
    while x8, local copies, waits for them, and re-layouts  9.79 us
  transfers between devices with their start and end apart: 12, of which 5 were waited for; matrix products, arithmetic and copies ran while one was open for 21% of the time, Pallas kernels for 0%

profile of v1, /device:TPU:0, one launch (start us, length us, event | category | flops | bytes accessed | tf_op | source)
XLA Modules:
  0.0 252.2 jit_solution(11233399093312790226)
XLA Ops:
  0.7 3.6 %reshape.224 = f32[256,2,1024]{2,1,0:T(2,128)} reshape(bf16[1,512,1024]{2,1,0:T(8,128)(2,1)} %param.11) | data formatting | bytes 3145728 | tf_op jit(solution)/shard_map/convert_element_type | solution.py:75
  4.2 5.1 %reduce_sum.74 = f32[256,1024]{1,0:T(8,128)} reduce(f32[256,2,1024]{2,1,0:T(2,128)} %reshape.224, f32[]{:T(128)} %constant.128.clone.1), dimensions={1}, to_apply=%region_0.0 | reduce | flops 262144 | bytes 3145732 | tf_op jit(solution)/shard_map/reduce_sum | solution.py:75
  13.4 7.3 %all-to-all-start.1 = ((bf16[256,8,128]{0,2,1:T(8,128)(2,1)}), bf16[256,8,128]{0,2,1:T(8,128)(2,1)}, u32[]{:S(2)}, u32[]{:S(2)}) async-start(bf16[256,8,128]{0,2,1:T(8,128)(2,1)} %bitcast.157), calls=%async_computation.1 | async-start | bytes 1048576 | tf_op jit(solution)/shard_map/all_to_all | solution.py:81
  22.1 3.5 %reshape.225 = f32[256,2,1024]{2,1,0:T(2,128)} reshape(bf16[1,512,1024]{2,1,0:T(8,128)(2,1)} %param.10) | data formatting | bytes 3145728 | tf_op jit(solution)/shard_map/convert_element_type | solution.py:72
  25.5 5.1 %reduce_sum.75 = f32[256,1024]{1,0:T(8,128)} reduce(f32[256,2,1024]{2,1,0:T(2,128)} %reshape.225, f32[]{:T(128)} %constant.128.clone.1), dimensions={1}, to_apply=%region_1.0 | reduce | flops 262144 | bytes 3145732 | tf_op jit(solution)/shard_map/reduce_sum | solution.py:72
  44.9 5.3 %divide_convert_fusion = bf16[256,16,64]{0,2,1:T(8,128)(2,1)S(1)} fusion(bf16[512,16,64]{0,2,1:T(8,128)(2,1)} %bitcast.160, f32[16,256,512]{2,1,0:T(8,128)} %copy-done.3, f32[256,16]{0,1:T(8,128)S(1)} %get-tuple-element.79, f32[256,16]{0,1:T(8,128)S(1)} %fusion.16), kind=kOutput, calls=%fused_computation.31 | convolution fusion | flops 275251200 | bytes 9994240 | tf_op jit(solution)/shard_map/nhm,mhe->nhe/dot_general | solution.py:47
  66.2 4.2 %all-to-all-start = ((bf16[512,8,128]{0,2,1:T(8,128)(2,1)}), bf16[512,8,128]{0,2,1:T(8,128)(2,1)}, u32[]{:S(2)}, u32[]{:S(2)}) async-start(bf16[512,8,128]{0,2,1:T(8,128)(2,1)} %bitcast.154), calls=%async_computation | async-start | bytes 2097152 | tf_op jit(solution)/shard_map/all_to_all | solution.py:80
  70.8 3.8 %collective-permute-start.5 = (bf16[256,128]{1,0:T(8,128)(2,1)S(1)}, bf16[256,128]{1,0:T(8,128)(2,1)S(1)}, u32[]{:S(2)}, u32[]{:S(2)}) collective-permute-start(bf16[256,128]{1,0:T(8,128)(2,1)S(1)} %bitcast.169), channel_id=1, source_target_pairs={{0,24},{4,28},{8,0},{12,4},{16,8},{20,12},{24,16},{28,20},{1,25},{... | collective-permute-start | bytes 196616 | tf_op jit(solution)/shard_map/ppermute | solution.py:31
  79.5 8.6 %collective-permute-done.5 = bf16[256,128]{1,0:T(8,128)(2,1)S(1)} collective-permute-done((bf16[256,128]{1,0:T(8,128)(2,1)S(1)}, bf16[256,128]{1,0:T(8,128)(2,1)S(1)}, u32[]{:S(2)}, u32[]{:S(2)}) %collective-permute-start.5) | collective-permute-done | bytes 65568 | tf_op jit(solution)/shard_map/ppermute | solution.py:31
  92.6 3.6 %all-to-all-done = bf16[512,8,128]{0,2,1:T(8,128)(2,1)} async-done(((bf16[512,8,128]{0,2,1:T(8,128)(2,1)}), bf16[512,8,128]{0,2,1:T(8,128)(2,1)}, u32[]{:S(2)}, u32[]{:S(2)}) %all-to-all-start) | async-done | bytes 1048608 | tf_op jit(solution)/shard_map/all_to_all | solution.py:80
  98.4 76.4 %while.11 = (s32[]{:T(128)}, bf16[4,1024,128]{2,1,0:T(8,128)(2,1)}, bf16[4,1024,128]{2,1,0:T(8,128)(2,1)}, bf16[2048,128]{0,1:T(8,128)(2,1)S(1)}, bf16[8,256,128...) while((s32[]{:T(128)}, bf16[4,1024,128]{2,1,0:T(8,128)(2,1)}, ...), condition=%wide.wide.region_7.8_spmd, body=%wide.wide.region_4.7_spmd.sunk | while | flops 1107554304 | bytes 121152104 | solution.py:60
  102.1 3.3 %fusion.75 = f32[1024,2]{0,1:T(2,128)S(1)} fusion(f32[2,1024,2048]{2,1,0:T(8,128)S(1)} %get-tuple-element.144, f32[1024,2]{0,1:T(2,128)S(1)} %get-tuple-element.145), kind=kLoop, calls=%fused_computation.7.clone.clone.1 | loop fusion | flops 12580864 | bytes 16793600 | tf_op jit(solution)/shard_map/while/body/eval_jaxpr/reduce_sum | solution.py:46
  107.8 8.8 %fusion.76 = bf16[1024,2,64]{0,2,1:T(8,128)(2,1)S(1)} fusion(bf16[2048,2,64]{0,2,1:T(8,128)(2,1)} %get-tuple-element.165, f32[2,1024,2048]{2,1,0:T(8,128)} %copy-done.2, f32[1024,2]{0,1:T(2,128)S(1)} %get-tuple-element.145, f32[1024,2]{0,1:T(2,128)S(1)} %fusion.75), kind=kOutput, calls=%fused_computation.12.clone.clone.1 | convolution fusion | flops 549715968 | bytes 17580032 | tf_op jit(solution)/shard_map/while/body/eval_jaxpr/nhm,mhe->nhe/dot_general | solution.py:47
  121.2 3.3 %fusion.75 = f32[1024,2]{0,1:T(2,128)S(1)} fusion(f32[2,1024,2048]{2,1,0:T(8,128)S(1)} %get-tuple-element.144, f32[1024,2]{0,1:T(2,128)S(1)} %get-tuple-element.145), kind=kLoop, calls=%fused_computation.7.clone.clone.1 | loop fusion | flops 12580864 | bytes 16793600 | tf_op jit(solution)/shard_map/while/body/eval_jaxpr/reduce_sum | solution.py:46
  126.9 8.8 %fusion.76 = bf16[1024,2,64]{0,2,1:T(8,128)(2,1)S(1)} fusion(bf16[2048,2,64]{0,2,1:T(8,128)(2,1)} %get-tuple-element.165, f32[2,1024,2048]{2,1,0:T(8,128)} %copy-done.2, f32[1024,2]{0,1:T(2,128)S(1)} %get-tuple-element.145, f32[1024,2]{0,1:T(2,128)S(1)} %fusion.75), kind=kOutput, calls=%fused_computation.12.clone.clone.1 | convolution fusion | flops 549715968 | bytes 17580032 | tf_op jit(solution)/shard_map/while/body/eval_jaxpr/nhm,mhe->nhe/dot_general | solution.py:47
  140.2 3.3 %fusion.75 = f32[1024,2]{0,1:T(2,128)S(1)} fusion(f32[2,1024,2048]{2,1,0:T(8,128)S(1)} %get-tuple-element.144, f32[1024,2]{0,1:T(2,128)S(1)} %get-tuple-element.145), kind=kLoop, calls=%fused_computation.7.clone.clone.1 | loop fusion | flops 12580864 | bytes 16793600 | tf_op jit(solution)/shard_map/while/body/eval_jaxpr/reduce_sum | solution.py:46
  146.0 8.8 %fusion.76 = bf16[1024,2,64]{0,2,1:T(8,128)(2,1)S(1)} fusion(bf16[2048,2,64]{0,2,1:T(8,128)(2,1)} %get-tuple-element.165, f32[2,1024,2048]{2,1,0:T(8,128)} %copy-done.2, f32[1024,2]{0,1:T(2,128)S(1)} %get-tuple-element.145, f32[1024,2]{0,1:T(2,128)S(1)} %fusion.75), kind=kOutput, calls=%fused_computation.12.clone.clone.1 | convolution fusion | flops 549715968 | bytes 17580032 | tf_op jit(solution)/shard_map/while/body/eval_jaxpr/nhm,mhe->nhe/dot_general | solution.py:47
  159.3 3.3 %fusion.75 = f32[1024,2]{0,1:T(2,128)S(1)} fusion(f32[2,1024,2048]{2,1,0:T(8,128)S(1)} %get-tuple-element.144, f32[1024,2]{0,1:T(2,128)S(1)} %get-tuple-element.145), kind=kLoop, calls=%fused_computation.7.clone.clone.1 | loop fusion | flops 12580864 | bytes 16793600 | tf_op jit(solution)/shard_map/while/body/eval_jaxpr/reduce_sum | solution.py:46
  165.0 8.8 %fusion.76 = bf16[1024,2,64]{0,2,1:T(8,128)(2,1)S(1)} fusion(bf16[2048,2,64]{0,2,1:T(8,128)(2,1)} %get-tuple-element.165, f32[2,1024,2048]{2,1,0:T(8,128)} %copy-done.2, f32[1024,2]{0,1:T(2,128)S(1)} %get-tuple-element.145, f32[1024,2]{0,1:T(2,128)S(1)} %fusion.75), kind=kOutput, calls=%fused_computation.12.clone.clone.1 | convolution fusion | flops 549715968 | bytes 17580032 | tf_op jit(solution)/shard_map/while/body/eval_jaxpr/nhm,mhe->nhe/dot_general | solution.py:47
  174.8 7.9 %all-to-all-start.2 = ((bf16[8,512,128]{2,1,0:T(8,128)(2,1)}), bf16[8,512,128]{2,1,0:T(8,128)(2,1)S(1)}, u32[]{:S(2)}, u32[]{:S(2)}) async-start(bf16[8,512,128]{2,1,0:T(8,128)(2,1)} %bitcast.159), calls=%async_computation.2 | async-start | bytes 2097152 | tf_op jit(solution)/shard_map/all_to_all | solution.py:86
  185.9 20.4 %all-to-all-done.2 = bf16[8,512,128]{2,1,0:T(8,128)(2,1)S(1)} async-done(((bf16[8,512,128]{2,1,0:T(8,128)(2,1)}), bf16[8,512,128]{2,1,0:T(8,128)(2,1)S(1)}, u32[]{:S(2)}, u32[]{:S(2)}) %all-to-all-start.2) | async-done | bytes 1048608 | tf_op jit(solution)/shard_map/all_to_all | solution.py:86
  206.3 3.2 %all-to-all-start.3 = ((bf16[4,2,128]{2,1,0:T(2,128)(2,1)}), bf16[4,2,128]{2,1,0:T(2,128)(2,1)S(1)}, u32[]{:S(2)}, u32[]{:S(2)}) async-start(bf16[4,2,128]{2,1,0:T(2,128)(2,1)} %select_convert_fusion), calls=%async_computation.3 | async-start | bytes 4096 | tf_op jit(solution)/shard_map/all_to_all | solution.py:118
  219.2 4.4 %all-to-all-start.4 = ((bf16[4,2,128,1024]{3,2,1,0:T(8,128)(2,1)}), bf16[4,2,128,1024]{3,2,1,0:T(8,128)(2,1)}, u32[]{:S(2)}, u32[]{:S(2)}) async-start(bf16[4,2,128,1024]{3,2,1,0:T(8,128)(2,1)} %select_select_fusion), calls=%async_computation.4 | async-start | bytes 4194304 | tf_op jit(solution)/shard_map/all_to_all | solution.py:117
  226.7 22.7 %all-to-all-done.4 = bf16[4,2,128,1024]{3,2,1,0:T(8,128)(2,1)} async-done(((bf16[4,2,128,1024]{3,2,1,0:T(8,128)(2,1)}), bf16[4,2,128,1024]{3,2,1,0:T(8,128)(2,1)}, u32[]{:S(2)}, u32[]{:S(2)}) %all-to-all-start.4) | async-done | bytes 2097184 | tf_op jit(solution)/shard_map/all_to_all | solution.py:117
  (132 shorter events, 93.9 us)
Async XLA Ops:
  0.6 210.4 %copy-start = (bf16[1024,1024]{1,0:T(8,128)(2,1)S(1)}, bf16[1024,1024]{1,0:T(8,128)(2,1)}, u32[]{:S(2)}) copy-start(bf16[1024,1024]{1,0:T(8,128)(2,1)} %param.13) | copy-start | bytes 6291460
  0.6 20.1 %copy-start.5 = (bf16[1,512,1024]{2,1,0:T(8,128)(2,1)S(1)}, bf16[1,512,1024]{2,1,0:T(8,128)(2,1)}, u32[]{:S(2)}) copy-start(bf16[1,512,1024]{2,1,0:T(8,128)(2,1)} %param.11) | copy-start | bytes 3145732
  13.4 52.8 %all-to-all-start.1 = ((bf16[256,8,128]{0,2,1:T(8,128)(2,1)}), bf16[256,8,128]{0,2,1:T(8,128)(2,1)}, u32[]{:S(2)}, u32[]{:S(2)}) async-start(bf16[256,8,128]{0,2,1:T(8,128)(2,1)} %bitcast.157), calls=%async_computation.1 | async-start | bytes 1048576 | tf_op jit(solution)/shard_map/all_to_all | solution.py:81
  22.1 12.7 %copy-start.7 = (bf16[1,512,1024]{1,2,0:T(8,128)(2,1)S(1)}, bf16[1,512,1024]{1,2,0:T(8,128)(2,1)}, u32[]{:S(2)}) copy-start(bf16[1,512,1024]{1,2,0:T(8,128)(2,1)} %copy.114) | copy-start | bytes 3145732
  42.5 22.3 %copy-start.6 = (bf16[1,512,1024]{2,1,0:T(8,128)(2,1)S(1)}, bf16[1,512,1024]{2,1,0:T(8,128)(2,1)}, u32[]{:S(2)}) copy-start(bf16[1,512,1024]{2,1,0:T(8,128)(2,1)} %param.10) | copy-start | bytes 3145732
  52.5 18.3 %collective-permute-start = (bf16[256,128]{1,0:T(8,128)(2,1)}, bf16[256,128]{1,0:T(8,128)(2,1)}, u32[]{:S(2)}, u32[]{:S(2)}) collective-permute-start(bf16[256,128]{1,0:T(8,128)(2,1)} %bitcast.167), channel_id=1, source_target_pairs={{0,4},{4,8},{8,12},{12,16},{16,20},{20,24},{24,28},{28,0},{1,5},{5... | collective-permute-start | bytes 196616 | tf_op jit(solution)/shard_map/ppermute | solution.py:31
  56.1 19.4 %collective-permute-start.1 = (bf16[256,128]{1,0:T(8,128)(2,1)}, bf16[256,128]{1,0:T(8,128)(2,1)}, u32[]{:S(2)}, u32[]{:S(2)}) collective-permute-start(bf16[256,128]{1,0:T(8,128)(2,1)} %bitcast.166), channel_id=1, source_target_pairs={{0,8},{4,12},{8,16},{12,20},{16,24},{20,28},{24,0},{28,4},{1,9},{5... | collective-permute-start | bytes 196616 | tf_op jit(solution)/shard_map/ppermute | solution.py:31
  58.3 19.5 %collective-permute-start.2 = (bf16[256,128]{1,0:T(8,128)(2,1)}, bf16[256,128]{1,0:T(8,128)(2,1)}, u32[]{:S(2)}, u32[]{:S(2)}) collective-permute-start(bf16[256,128]{1,0:T(8,128)(2,1)} %bitcast.165), channel_id=1, source_target_pairs={{0,12},{4,16},{8,20},{12,24},{16,28},{20,0},{24,4},{28,8},{1,13},{... | collective-permute-start | bytes 196616 | tf_op jit(solution)/shard_map/ppermute | solution.py:31
  60.7 17.9 %collective-permute-start.3 = (bf16[256,128]{1,0:T(8,128)(2,1)S(1)}, bf16[256,128]{1,0:T(8,128)(2,1)}, u32[]{:S(2)}, u32[]{:S(2)}) collective-permute-start(bf16[256,128]{1,0:T(8,128)(2,1)S(1)} %bitcast.164), channel_id=1, source_target_pairs={{0,16},{4,20},{8,24},{12,28},{16,0},{20,4},{24,8},{28,12},{1,17},{... | collective-permute-start | bytes 196616 | tf_op jit(solution)/shard_map/ppermute | solution.py:31
  62.4 17.1 %collective-permute-start.4 = (bf16[256,128]{1,0:T(8,128)(2,1)S(1)}, bf16[256,128]{1,0:T(8,128)(2,1)S(1)}, u32[]{:S(2)}, u32[]{:S(2)}) collective-permute-start(bf16[256,128]{1,0:T(8,128)(2,1)S(1)} %bitcast.163), channel_id=1, source_target_pairs={{0,20},{4,24},{8,28},{12,0},{16,4},{20,8},{24,12},{28,16},{1,21},{... | collective-permute-start | bytes 196616 | tf_op jit(solution)/shard_map/ppermute | solution.py:31
  66.2 29.9 %all-to-all-start = ((bf16[512,8,128]{0,2,1:T(8,128)(2,1)}), bf16[512,8,128]{0,2,1:T(8,128)(2,1)}, u32[]{:S(2)}, u32[]{:S(2)}) async-start(bf16[512,8,128]{0,2,1:T(8,128)(2,1)} %bitcast.154), calls=%async_computation | async-start | bytes 2097152 | tf_op jit(solution)/shard_map/all_to_all | solution.py:80
  70.8 17.4 %collective-permute-start.5 = (bf16[256,128]{1,0:T(8,128)(2,1)S(1)}, bf16[256,128]{1,0:T(8,128)(2,1)S(1)}, u32[]{:S(2)}, u32[]{:S(2)}) collective-permute-start(bf16[256,128]{1,0:T(8,128)(2,1)S(1)} %bitcast.169), channel_id=1, source_target_pairs={{0,24},{4,28},{8,0},{12,4},{16,8},{20,12},{24,16},{28,20},{1,25},{... | collective-permute-start | bytes 196616 | tf_op jit(solution)/shard_map/ppermute | solution.py:31
  75.4 13.5 %collective-permute-start.6 = (bf16[256,128]{1,0:T(8,128)(2,1)S(1)}, bf16[256,128]{1,0:T(8,128)(2,1)S(1)}, u32[]{:S(2)}, u32[]{:S(2)}) collective-permute-start(bf16[256,128]{1,0:T(8,128)(2,1)S(1)} %bitcast.168), channel_id=1, source_target_pairs={{0,28},{4,0},{8,4},{12,8},{16,12},{20,16},{24,20},{28,24},{1,29},{... | collective-permute-start | bytes 196616 | tf_op jit(solution)/shard_map/ppermute | solution.py:31
  98.4 84.3 %copy-start.12 = (s32[1,4,1]{1,2,0:T(1,128)S(1)}, s32[1,4,1]{1,2,0:T(1,128)}, u32[]{:S(2)}) copy-start(s32[1,4,1]{1,2,0:T(1,128)} %param.15) | copy-start | bytes 52
  98.4 85.0 %copy-start.1 = (s32[1,4]{1,0:T(1,128)S(1)}, s32[1,4]{1,0:T(1,128)}, u32[]{:S(2)}) copy-start(s32[1,4]{1,0:T(1,128)} %param.16) | copy-start | bytes 52
  98.4 86.3 %copy-start.10 = (s32[1,4,128]{2,1,0:T(4,128)S(1)}, s32[1,4,128]{2,1,0:T(4,128)}, u32[]{:S(2)}) copy-start(s32[1,4,128]{2,1,0:T(4,128)} %param.17) | copy-start | bytes 6148
  102.1 5.7 %copy-start.2 = (f32[2,1024,2048]{2,1,0:T(8,128)}, f32[2,1024,2048]{2,1,0:T(8,128)S(1)}, u32[]{:S(2)}) copy-start(f32[2,1024,2048]{2,1,0:T(8,128)S(1)} %get-tuple-element.144) | copy-start | bytes 50331652 | tf_op jit(solution)/shard_map/while
  121.2 5.7 %copy-start.2 = (f32[2,1024,2048]{2,1,0:T(8,128)}, f32[2,1024,2048]{2,1,0:T(8,128)S(1)}, u32[]{:S(2)}) copy-start(f32[2,1024,2048]{2,1,0:T(8,128)S(1)} %get-tuple-element.144) | copy-start | bytes 50331652 | tf_op jit(solution)/shard_map/while
  140.2 5.7 %copy-start.2 = (f32[2,1024,2048]{2,1,0:T(8,128)}, f32[2,1024,2048]{2,1,0:T(8,128)S(1)}, u32[]{:S(2)}) copy-start(f32[2,1024,2048]{2,1,0:T(8,128)S(1)} %get-tuple-element.144) | copy-start | bytes 50331652 | tf_op jit(solution)/shard_map/while
  159.3 5.7 %copy-start.2 = (f32[2,1024,2048]{2,1,0:T(8,128)}, f32[2,1024,2048]{2,1,0:T(8,128)S(1)}, u32[]{:S(2)}) copy-start(f32[2,1024,2048]{2,1,0:T(8,128)S(1)} %get-tuple-element.144) | copy-start | bytes 50331652 | tf_op jit(solution)/shard_map/while
  174.8 39.0 %copy-start.11 = (f32[1024]{0:T(1024)S(1)}, f32[1024]{0:T(1024)}, u32[]{:S(2)}) copy-start(f32[1024]{0:T(1024)} %param.14) | copy-start | bytes 12292
  174.8 31.5 %all-to-all-start.2 = ((bf16[8,512,128]{2,1,0:T(8,128)(2,1)}), bf16[8,512,128]{2,1,0:T(8,128)(2,1)S(1)}, u32[]{:S(2)}, u32[]{:S(2)}) async-start(bf16[8,512,128]{2,1,0:T(8,128)(2,1)} %bitcast.159), calls=%async_computation.2 | async-start | bytes 2097152 | tf_op jit(solution)/shard_map/all_to_all | solution.py:86
  206.3 12.9 %all-to-all-start.3 = ((bf16[4,2,128]{2,1,0:T(2,128)(2,1)}), bf16[4,2,128]{2,1,0:T(2,128)(2,1)S(1)}, u32[]{:S(2)}, u32[]{:S(2)}) async-start(bf16[4,2,128]{2,1,0:T(2,128)(2,1)} %select_convert_fusion), calls=%async_computation.3 | async-start | bytes 4096 | tf_op jit(solution)/shard_map/all_to_all | solution.py:118
  219.2 30.2 %all-to-all-start.4 = ((bf16[4,2,128,1024]{3,2,1,0:T(8,128)(2,1)}), bf16[4,2,128,1024]{3,2,1,0:T(8,128)(2,1)}, u32[]{:S(2)}, u32[]{:S(2)}) async-start(bf16[4,2,128,1024]{3,2,1,0:T(8,128)(2,1)} %select_select_fusion), calls=%async_computation.4 | async-start | bytes 4194304 | tf_op jit(solution)/shard_map/all_to_all | solution.py:117
  (4 other events, 10.2 us)
